TPU v7x, 32 devices: a whole 2x2x4 slice. The times are simulated.
32 devices in a mesh: member: 2 (over x), ty: 16 (over z, y, core).
Axes of the slice: x: 2, y: 2, z: 4, core: 2. Of those that a mesh axis runs over, the one named last changes fastest.
Arguments:
- fields: float32 [32, 768, 6, 768], P('member', 'ty'), parts along dimension 0, may hold values from -6 to 6
- damp_four: float32 [32], P('member'), parts along dimension 0, may hold values from 0.004 to 0.03
- damp_six: float32 [32], P('member'), parts along dimension 0, may hold values from 0.0008 to 0.006
- metric: float32 [4, 768, 6, 768], P(None, 'ty'), may hold values from 0.1 to 1.9
- seam_table: int32 [6, 4, 3], replicated, may hold values from 0 to 5
Outputs:
- damped: float32 [32, 768, 6, 768], P('member', 'ty'), parts along dimension 0
There are 2 independent parts, one for each index of `member`. A program takes and returns all parts, laid end to end along the dimension named above; an argument that names none is the same for every part. Nothing has to cross between parts.
Inputs may be any that keep to these rules, and one draw needn't show every extreme that they name: The table describes the surface of a cube with every face seen from outside: the joining is symmetric, no face is joined to itself, and r is 1 exactly when both edges are among (south, east) or both among (north, west).
All inputs are finite; a program needn't handle non-finite values.
Results may differ from a plain program's by a relative error of at most 0.00005.
Values sent between devices are 32-bit elements; how exact they have to be, the bound alone decides.
A program may use at most 128 MiB of HBM per device.

v0:
```python
import jax
import jax.numpy as jnp
from jax import lax
from jax.sharding import PartitionSpec as P


def with_halo(cells, sides, width):
    for axis, dim in sides:
        count = lax.axis_size(axis)
        ends = count - 1
        head = lax.slice_in_dim(cells, 0, width, axis=dim)
        tail = lax.slice_in_dim(cells, cells.shape[dim] - width, cells.shape[dim], axis=dim)
        cells = jnp.concatenate(
            [
                lax.ppermute(tail, axis, [(i, (i + 1) % count) for i in range(ends)]),
                cells,
                lax.ppermute(head, axis, [((i + 1) % count, i) for i in range(ends)]),
            ],
            axis=dim,
        )
    return cells


def strip_edges(source):
    east_cells = jnp.transpose(source[:, :, :, -1], (0, 2, 1))
    west_cells = jnp.transpose(source[:, :, :, 0], (0, 2, 1))
    return jnp.stack([east_cells, west_cells], axis=2)


def gather_edges(source):
    tile_index = lax.axis_index("ty")
    tile_count = lax.axis_size("ty")
    strip_rows = source.shape[1]
    row_width = source.shape[3]
    strip_cells = strip_edges(source)
    first_row = jnp.where(tile_index == 0, source[:, 0], 0.0)
    last_row = jnp.where(tile_index == tile_count - 1, source[:, -1], 0.0)
    blank = jnp.zeros(strip_cells.shape[:3] + (row_width,), jnp.float32)
    placed = lax.dynamic_update_slice_in_dim(blank, strip_cells, tile_index * strip_rows, 3)
    rim_cells = jnp.stack([first_row, placed[:, :, 0], last_row, placed[:, :, 1]], axis=2)
    edge_set = lax.psum(rim_cells, "ty")
    return edge_set


def seam_halo(edge_set, seam_table):
    levels = edge_set.shape[0]
    row_width = edge_set.shape[3]
    flattened = edge_set.reshape(levels, 24, row_width)
    picked = (seam_table[:, :, 0] * 4 + seam_table[:, :, 1]).reshape(24)
    onehot = (picked[:, None] == jnp.arange(24, dtype=jnp.int32)[None, :]).astype(jnp.float32)
    neighbor = jnp.einsum("jk,lkc->ljc", onehot, flattened, precision=lax.Precision.HIGHEST)
    neighbor = neighbor.reshape(levels, 6, 4, row_width)
    flipped = (seam_table[:, :, 2] == 1)[None, :, :, None]
    return jnp.where(flipped, neighbor[..., ::-1], neighbor)


def laplace(source, metric, seam_table):
    tile_index = lax.axis_index("ty")
    tile_count = lax.axis_size("ty")
    strip_rows = source.shape[1]
    padded = with_halo(source, (("ty", 1),), 1)
    halo_cells = seam_halo(gather_edges(source), seam_table)
    south_row = jnp.where(tile_index == 0, halo_cells[:, :, 0], padded[:, 0])
    north_row = jnp.where(tile_index == tile_count - 1, halo_cells[:, :, 2], padded[:, -1])
    row_start = tile_index * strip_rows
    west_cells = jnp.transpose(
        lax.dynamic_slice_in_dim(halo_cells[:, :, 3], row_start, strip_rows, 2), (0, 2, 1)
    )[..., None]
    east_cells = jnp.transpose(
        lax.dynamic_slice_in_dim(halo_cells[:, :, 1], row_start, strip_rows, 2), (0, 2, 1)
    )[..., None]
    padded_x = jnp.concatenate([west_cells, source, east_cells], axis=3)
    padded_y = jnp.concatenate([south_row[:, None], source, north_row[:, None]], axis=1)
    return (
        metric[0] * (padded_x[..., :-2] - source)
        + metric[1] * (padded_x[..., 2:] - source)
        + metric[2] * (padded_y[:, :-2] - source)
        + metric[3] * (padded_y[:, 2:] - source)
    )


def per_device(fields, damp_four, damp_six, metric, seam_table):
    second = laplace(fields, metric, seam_table)
    fourth = laplace(second, metric, seam_table)
    sixth = laplace(fourth, metric, seam_table)
    return fields - damp_four[:, None, None, None] * fourth + damp_six[:, None, None, None] * sixth


def solution(mesh):
    placed = (
        P("member", "ty", None, None),
        P("member"),
        P("member"),
        P(None, "ty", None, None),
        P(),
    )
    return jax.shard_map(
        per_device,
        mesh=mesh,
        in_specs=placed,
        out_specs=P("member", "ty", None, None),
        check_vma=False,
    )
```

profile of v0, /device:TPU:0, one launch (start us, length us, event | category | flops | bytes accessed | tf_op | source)
XLA Modules:
  0.0 596.8 jit_solution(6882728278029485408)
XLA Ops:
  6.5 4.6 fusion.54
  11.1 18.5 %copy.89 = f32[16,48,6,768]{3,0,2,1:T(8,128)} copy(f32[16,48,6,768]{3,1,2,0:T(8,128)} %param.5) | data formatting | bytes 28311552 | tf_op args[0]
  38.1 4.7 collective-permute-start
  49.8 88.0 %all-reduce.4.cloned.1.call-done = f32[16,24,768]{2,1,0:T(8,128)} async-done(((f32[16,24,768]{2,1,0:T(8,128)}), f32[16,24,768]{2,1,0:T(8,128)}) %all-reduce.4.cloned.1.call-update) | async-done | bytes 1179664 | tf_op jit(solution)/shard_map/psum | solution.py:41
  141.1 4.7 rev.9
  150.1 3.9 copy.68
  155.7 4.0 copy.73
  161.7 33.4 %fusion.26 = f32[16,48,6,768]{3,0,2,1:T(8,128)} fusion(f32[16,48,6,768]{3,0,2,1:T(8,128)} %copy.89, f32[16,1,6,768]{3,0,2,1:T(8,128)} %get-tuple-element.38, f32[16,1,6,768]{3,0,2,1:T(8,128)} %get-tuple-element.37, f32[16,48,6,1]{3,0,2,1:T(8,128)} %copy.73, f32[16,48,6,1]{3,0,2,1:T(8,128)} %copy.68, f32[48,6,768]{2,1,0:T(8,128)} %copy.79, ...), kind=kLoop, calls=%fused_computation.35 | loop fusion | flops 53084160 | bytes 32477184 | tf_op jit(solution)/shard_map/add | solution.py:75
  195.1 5.3 fusion.52
  202.5 3.4 copy.104
  205.9 3.4 copy.83
  220.1 3.2 collective-permute-start.2
  224.6 91.8 %all-reduce.6.cloned.1.call-done = f32[16,24,768]{2,1,0:T(8,128)} async-done(((f32[16,24,768]{2,1,0:T(8,128)}), f32[16,24,768]{2,1,0:T(8,128)}) %all-reduce.6.cloned.1.call-update) | async-done | bytes 1179664 | tf_op jit(solution)/shard_map/psum | solution.py:41
  316.4 3.0 convolution_bitcast_fusion.1
  319.3 10.9 %reshape.133 = f32[16,6,4,768]{3,2,1,0:T(4,128)} reshape(f32[16,24,768]{2,1,0:T(8,128)} %convolution_bitcast_fusion.1) | data formatting | bytes 2359296 | tf_op jit(solution)/shard_map/reshape | solution.py:52
  330.3 2.7 copy.85
  332.9 4.7 rev.10
  342.1 3.9 copy.87
  347.7 4.0 copy.88
  353.7 34.7 %fusion.15 = f32[16,48,6,768]{3,0,2,1:T(8,128)} fusion(f32[16,48,6,768]{3,0,2,1:T(8,128)} %fusion.26, f32[16,1,6,768]{3,0,2,1:T(8,128)} %get-tuple-element.34, f32[16,1,6,768]{3,0,2,1:T(8,128)} %get-tuple-element.33, f32[16,48,6,1]{3,0,2,1:T(8,128)} %copy.88, f32[16,48,6,1]{3,0,2,1:T(8,128)} %copy.87, f32[48,6,768]{2,1,0:T(8,128)} %copy.79, ...), kind=kLoop, calls=%fused_computation.20 | loop fusion | flops 53084160 | bytes 32477184 | tf_op jit(solution)/shard_map/add | solution.py:75
  388.4 5.3 fusion.50
  395.8 3.4 copy.90
  399.2 3.4 copy.91
  410.7 2.8 reshape.134
  413.6 3.2 collective-permute-start.4
  418.1 91.7 %all-reduce.8.cloned.1.call-done = f32[16,24,768]{2,1,0:T(8,128)} async-done(((f32[16,24,768]{2,1,0:T(8,128)}), f32[16,24,768]{2,1,0:T(8,128)}) %all-reduce.8.cloned.1.call-update) | async-done | bytes 1179664 | tf_op jit(solution)/shard_map/psum | solution.py:41
  509.8 3.0 convolution_bitcast_fusion
  518.0 4.7 rev.11
  526.5 3.9 copy.97
  530.5 4.0 copy.98
  536.0 35.3 %fusion.4 = f32[16,48,6,768]{3,0,2,1:T(8,128)} fusion(f32[16,48,6,768]{3,0,2,1:T(8,128)} %fusion.15, f32[16,1,6,768]{3,0,2,1:T(8,128)S(1)} %get-tuple-element.30, f32[16,1,6,768]{3,0,2,1:T(8,128)S(1)} %get-tuple-element.29, f32[16,48,6,1]{3,0,2,1:T(8,128)} %copy.98, f32[16,48,6,1]{3,0,2,1:T(8,128)} %copy.97, f32[16]{0:T(128)S(1)} %copy-done.5, ...), kind=kLoop, calls=%fused_computation.5 | loop fusion | flops 67239936 | bytes 46633088 | tf_op jit(solution)/shard_map/add | solution.py:86
  571.3 18.5 %copy.99 = f32[16,48,6,768]{3,1,2,0:T(8,128)} copy(f32[16,48,6,768]{3,0,2,1:T(8,128)} %fusion.4) | data formatting | bytes 28311552 | tf_op jit(solution)/shard_map/add | solution.py:86
  (83 shorter events, 70.8 us)
Async XLA Ops:
  6.5 131.3 %all-reduce.4.cloned.1.call-start = ((), (), s32[]{:S(2)}) async-start(), calls=%async_computation | async-start | bytes 2359296 | tf_op jit(solution)/shard_map/psum | solution.py:41
  36.6 7.5 %copy-start.4 = (s32[6,4,3]{0,1,2:T(4,128)S(1)}, s32[6,4,3]{0,1,2:T(4,128)}, u32[]{:S(2)}) copy-start(s32[6,4,3]{0,1,2:T(4,128)} %param.9) | copy-start | bytes 868
  38.0 278.3 %all-reduce.6.cloned.1.call-start = ((), (), s32[]{:S(2)}) async-start(), calls=%async_computation.1 | async-start | bytes 2359296 | tf_op jit(solution)/shard_map/psum | solution.py:41
  38.1 121.6 %collective-permute-start = (f32[16,1,6,768]{3,0,2,1:T(8,128)}, f32[16,1,6,768]{3,0,2,1:T(8,128)}, u32[]{:S(2)}, u32[]{:S(2)}) collective-permute-start(f32[16,1,6,768]{3,0,2,1:T(8,128)} %get-tuple-element.17), channel_id=1, source_target_pairs={{0,1},{1,2},{2,3},{3,4},{4,5},{5,6},{6,7},{7,8},{8,9},{9,10},{10,1... | collective-permute-start | bytes 884744 | tf_op jit(solution)/shard_map/ppermute | solution.py:15
  42.8 116.8 %collective-permute-start.1 = (f32[16,1,6,768]{3,0,2,1:T(8,128)}, f32[16,1,6,768]{3,0,2,1:T(8,128)}, u32[]{:S(2)}, u32[]{:S(2)}) collective-permute-start(f32[16,1,6,768]{3,0,2,1:T(8,128)} %get-tuple-element.19), channel_id=1, source_target_pairs={{1,0},{2,1},{3,2},{4,3},{5,4},{6,5},{7,6},{8,7},{9,8},{10,9},{11,1... | collective-permute-start | bytes 884744 | tf_op jit(solution)/shard_map/ppermute | solution.py:17
  147.7 1.0 copy-start.2
  220.0 289.8 %all-reduce.8.cloned.1.call-start = ((), (), s32[]{:S(2)}) async-start(), calls=%async_computation.2 | async-start | bytes 2359296 | tf_op jit(solution)/shard_map/psum | solution.py:41
  220.1 131.6 %collective-permute-start.2 = (f32[16,1,6,768]{3,0,2,1:T(8,128)}, f32[16,1,6,768]{3,0,2,1:T(8,128)}, u32[]{:S(2)}, u32[]{:S(2)}) collective-permute-start(f32[16,1,6,768]{3,0,2,1:T(8,128)} %get-tuple-element.11), channel_id=1, source_target_pairs={{0,1},{1,2},{2,3},{3,4},{4,5},{5,6},{6,7},{7,8},{8,9},{9,10},{10,1... | collective-permute-start | bytes 884744 | tf_op jit(solution)/shard_map/ppermute | solution.py:15
  223.3 128.3 %collective-permute-start.3 = (f32[16,1,6,768]{3,0,2,1:T(8,128)}, f32[16,1,6,768]{3,0,2,1:T(8,128)}, u32[]{:S(2)}, u32[]{:S(2)}) collective-permute-start(f32[16,1,6,768]{3,0,2,1:T(8,128)} %get-tuple-element.14), channel_id=1, source_target_pairs={{1,0},{2,1},{3,2},{4,3},{5,4},{6,5},{7,6},{8,7},{9,8},{10,9},{11,1... | collective-permute-start | bytes 884744 | tf_op jit(solution)/shard_map/ppermute | solution.py:17
  339.7 1.0 copy-start.3
  413.6 120.9 %collective-permute-start.4 = (f32[16,1,6,768]{3,0,2,1:T(8,128)}, f32[16,1,6,768]{3,0,2,1:T(8,128)}, u32[]{:S(2)}, u32[]{:S(2)}) collective-permute-start(f32[16,1,6,768]{3,0,2,1:T(8,128)} %get-tuple-element.5), channel_id=1, source_target_pairs={{0,1},{1,2},{2,3},{3,4},{4,5},{5,6},{6,7},{7,8},{8,9},{9,10},{10,1... | collective-permute-start | bytes 884744 | tf_op jit(solution)/shard_map/ppermute | solution.py:15
  416.8 117.7 %collective-permute-start.5 = (f32[16,1,6,768]{3,0,2,1:T(8,128)}, f32[16,1,6,768]{3,0,2,1:T(8,128)}, u32[]{:S(2)}, u32[]{:S(2)}) collective-permute-start(f32[16,1,6,768]{3,0,2,1:T(8,128)} %get-tuple-element.8), channel_id=1, source_target_pairs={{1,0},{2,1},{3,2},{4,3},{5,4},{6,5},{7,6},{8,7},{9,8},{10,9},{11,1... | collective-permute-start | bytes 884744 | tf_op jit(solution)/shard_map/ppermute | solution.py:17
  524.7 1.0 copy-start.1
  530.5 5.4 copy-start.5
  530.5 5.4 copy-start.6
  534.5 1.5 copy-start
Sparse Core Ops, SparseCore 0:
  38.2 99.5 all-reduce.3
  220.1 96.1 all-reduce.5
  413.7 96.0 all-reduce.7
where the time goes:
time: 606 us; the launch traced here: 597 us
  waiting for transfers between devices  271 us (45%)
  local copies, waits for them, and re-layouts  162 us (27%)
  other arithmetic  126 us (21%)
  starting transfers between devices  15.1 us (2%)
  between operations  13.8 us (2%)
  matrix products  7.85 us (1%)
    psum x3, waiting for transfers between devices, gather_edges(): edge_set = lax.psum(rim_cells, 'ty')  271 us
    add x2, other arithmetic, laplace(): metric[0] * (padded_x[..., :-2] - source)  68.1 us
    add x1, other arithmetic, per_device(): fields - damp_four[:, None, None, None] * fourth  35.3 us
    unnamed x19, local copies, waits for them, and re-layouts  28.6 us
    reshape x5, local copies, waits for them, and re-layouts, seam_halo(): neighbor = neighbor.reshape(levels, 6, 4, row_width)  20.2 us
    slice x4, local copies, waits for them, and re-layouts, strip_edges(): east_cells = jnp.transpose(source[:, :, :, -1], (0, 2, 1))  18.6 us
    add x1, local copies, waits for them, and re-layouts, per_device(): fields - damp_four[:, None, None, None] * fourth  18.5 us
    broadcast_in_dim x6, local copies, waits for them, and re-layouts, laplace(): jnp.transpose(lax.dynamic_slice_in_dim(halo_cells[:, :, 1], row_start, st...  15.9 us
  transfers between devices with their start and end apart: 9, of which 3 were waited for; matrix products, arithmetic and copies ran while one was open for 14% of the time, Pallas kernels for 0%

commit v1 on v0

--- a/solution.py
+++ b/solution.py
@@ -38,7 +38,10 @@
     blank = jnp.zeros(strip_cells.shape[:3] + (row_width,), jnp.float32)
     placed = lax.dynamic_update_slice_in_dim(blank, strip_cells, tile_index * strip_rows, 3)
     rim_cells = jnp.stack([first_row, placed[:, :, 0], last_row, placed[:, :, 1]], axis=2)
-    edge_set = lax.psum(rim_cells, "ty")
+    ndev = lax.axis_size("ty")
+    edge_set = rim_cells
+    for jj in [[(tick, tick ^ p) for tick in range(ndev)] for p in (1, 2, 4, 8, 16) if p < ndev]:
+        edge_set = edge_set + lax.ppermute(edge_set, "ty", perm=jj)
     return edge_set
 
 

time: 606 us -> 628 us (1.036)
  starting transfers between devices: 15.1 us -> 43.5 us
  waiting for transfers between devices: 271 us -> 292 us
  local copies, waits for them, and re-layouts: 162 us -> 145 us
  between operations: 13.8 us -> 0.75 us
    ppermute x0 -> x12, waiting for transfers between devices: none -> 292 us  [gather_edges(): edge_set = edge_set + lax.ppermute(edge_set, 'ty', perm=jj)]
    psum x3 -> x0, waiting for transfers between devices: 271 us -> none  [gather_edges(): edge_set = lax.psum(rim_cells, 'ty')]
    ppermute x0 -> x12, starting transfers between devices: none -> 23.4 us  [gather_edges(): edge_set = edge_set + lax.ppermute(edge_set, 'ty', perm=jj)]
    ppermute x3, starting transfers between devices: 3.84 us -> 14.1 us  [with_halo(): lax.ppermute(head, axis, [((i + 1) % count, i) for i in range(ends)])]
    reshape x3 -> x0, local copies, waits for them, and re-layouts: 6.85 us -> none  [seam_halo(): flattened = edge_set.reshape(levels, 24, row_width)]
    reshape x5 -> x6, local copies, waits for them, and re-layouts: 20.2 us -> 15.8 us  [seam_halo(): neighbor = neighbor.reshape(levels, 6, 4, row_width)]
    unnamed x19 -> x28, local copies, waits for them, and re-layouts: 28.6 us -> 28.6 us
  transfers between devices with their start and end apart: 9 -> 18, of which waited for: 3 -> 12; matrix products, arithmetic and copies ran while one was open for 14% -> 13% of each run, Pallas kernels for 0% -> 0%
where the time goes in v1:
time: 628 us; the launch traced here: 618 us
  waiting for transfers between devices  292 us (46%)
  local copies, waits for them, and re-layouts  145 us (23%)
  other arithmetic  129 us (21%)
  starting transfers between devices  43.5 us (7%)
  matrix products  7.07 us (1%)
    ppermute x12, waiting for transfers between devices, gather_edges(): edge_set = edge_set + lax.ppermute(edge_set, 'ty', perm=jj)  292 us
    add x2, other arithmetic, laplace(): metric[0] * (padded_x[..., :-2] - source)  68.3 us
    add x1, other arithmetic, per_device(): fields - damp_four[:, None, None, None] * fourth  35.4 us
    unnamed x28, local copies, waits for them, and re-layouts  28.6 us
    ppermute x12, starting transfers between devices, gather_edges(): edge_set = edge_set + lax.ppermute(edge_set, 'ty', perm=jj)  23.4 us
    slice x4, local copies, waits for them, and re-layouts, strip_edges(): east_cells = jnp.transpose(source[:, :, :, -1], (0, 2, 1))  18.6 us
    add x1, local copies, waits for them, and re-layouts, per_device(): fields - damp_four[:, None, None, None] * fourth  18.5 us
    broadcast_in_dim x6, local copies, waits for them, and re-layouts, laplace(): jnp.transpose(lax.dynamic_slice_in_dim(halo_cells[:, :, 1], row_start, st...  15.9 us
  transfers between devices with their start and end apart: 18, of which 12 were waited for; matrix products, arithmetic and copies ran while one was open for 13% of the time, Pallas kernels for 0%

profile of v1, /device:TPU:0, one launch (start us, length us, event | category | flops | bytes accessed | tf_op | source)
XLA Modules:
  0.0 617.7 jit_solution(9163846853558585950)
XLA Ops:
  0.0 4.6 fusion.60
  4.6 18.5 %copy.87 = f32[16,48,6,768]{3,0,2,1:T(8,128)} copy(f32[16,48,6,768]{3,1,2,0:T(8,128)} %param.5) | data formatting | bytes 28311552 | tf_op args[0]
  33.8 2.9 collective-permute-start.1
  36.7 26.3 %collective-permute-done.1 = f32[16,6,4,768]{3,0,2,1:T(8,128)S(1)} collective-permute-done((f32[16,6,4,768]{3,0,2,1:T(8,128)S(1)}, f32[16,6,4,768]{3,0,2,1:T(8,128)S(1)}, u32[]{:S(2)}, u32[]{:S(2)}) %collective-permute-start.1) | collective-permute-done | bytes 1179680 | tf_op jit(solution)/shard_map/ppermute | solution.py:44
  65.2 25.6 %collective-permute-done.2 = f32[16,6,4,768]{3,0,2,1:T(8,128)S(1)} collective-permute-done((f32[16,6,4,768]{3,0,2,1:T(8,128)S(1)}, f32[16,6,4,768]{3,0,2,1:T(8,128)S(1)}, u32[]{:S(2)}, u32[]{:S(2)}) %collective-permute-start.2) | collective-permute-done | bytes 1179680 | tf_op jit(solution)/shard_map/ppermute | solution.py:44
  101.7 43.3 %collective-permute-done.3 = f32[16,6,4,768]{3,0,2,1:T(8,128)} collective-permute-done((f32[16,6,4,768]{3,0,2,1:T(8,128)}, f32[16,6,4,768]{3,0,2,1:T(8,128)}, u32[]{:S(2)}, u32[]{:S(2)}) %collective-permute-start.3) | collective-permute-done | bytes 1179680 | tf_op jit(solution)/shard_map/ppermute | solution.py:44
  154.4 4.7 rev.9
  163.6 4.0 copy.65
  169.2 4.0 copy.70
  175.2 33.6 %fusion.26 = f32[16,48,6,768]{3,0,2,1:T(8,128)} fusion(f32[16,48,6,768]{3,0,2,1:T(8,128)} %copy.87, f32[16,1,6,768]{3,0,2,1:T(8,128)} %get-tuple-element.38, f32[16,1,6,768]{3,0,2,1:T(8,128)} %get-tuple-element.37, f32[16,48,6,1]{3,0,2,1:T(8,128)} %copy.70, f32[16,48,6,1]{3,0,2,1:T(8,128)} %copy.65, f32[48,6,768]{2,1,0:T(8,128)} %copy.75, ...), kind=kLoop, calls=%fused_computation.35 | loop fusion | flops 53084160 | bytes 32477184 | tf_op jit(solution)/shard_map/add | solution.py:78
  208.8 5.3 fusion.58
  216.3 3.4 copy.99
  219.7 3.4 copy.79
  234.4 26.3 %collective-permute-done.7 = f32[16,6,4,768]{3,0,1,2:T(8,128)S(1)} collective-permute-done((f32[16,6,4,768]{3,0,1,2:T(8,128)S(1)}, f32[16,6,4,768]{3,0,1,2:T(8,128)S(1)}, u32[]{:S(2)}, u32[]{:S(2)}) %collective-permute-start.7) | collective-permute-done | bytes 1179680 | tf_op jit(solution)/shard_map/ppermute | solution.py:44
  262.1 26.4 %collective-permute-done.8 = f32[16,6,4,768]{3,0,1,2:T(8,128)S(1)} collective-permute-done((f32[16,6,4,768]{3,0,1,2:T(8,128)S(1)}, f32[16,6,4,768]{3,0,1,2:T(8,128)S(1)}, u32[]{:S(2)}, u32[]{:S(2)}) %collective-permute-start.8) | collective-permute-done | bytes 1179680 | tf_op jit(solution)/shard_map/ppermute | solution.py:44
  293.1 11.0 %collective-permute-start.11 = (f32[16,1,6,768]{3,0,2,1:T(8,128)}, f32[16,1,6,768]{3,0,2,1:T(8,128)}, u32[]{:S(2)}, u32[]{:S(2)}) collective-permute-start(f32[16,1,6,768]{3,0,2,1:T(8,128)} %get-tuple-element.14), channel_id=1, source_target_pairs={{1,0},{2,1},{3,2},{4,3},{5,4},{6,5},{7,6},{8,7},{9,8},{10,9},{11,1... | collective-permute-start | bytes 884744 | tf_op jit(solution)/shard_map/ppermute | solution.py:17
  304.1 37.3 %collective-permute-done.9 = f32[16,6,4,768]{3,0,1,2:T(8,128)S(1)} collective-permute-done((f32[16,6,4,768]{3,0,1,2:T(8,128)S(1)}, f32[16,6,4,768]{3,0,1,2:T(8,128)S(1)}, u32[]{:S(2)}, u32[]{:S(2)}) %collective-permute-start.9) | collective-permute-done | bytes 1179680 | tf_op jit(solution)/shard_map/ppermute | solution.py:44
  349.3 4.8 rev.10
  358.5 4.0 copy.85
  364.1 4.0 copy.86
  370.1 34.7 %fusion.15 = f32[16,48,6,768]{3,0,2,1:T(8,128)} fusion(f32[16,48,6,768]{3,0,2,1:T(8,128)} %fusion.26, f32[16,1,6,768]{3,0,2,1:T(8,128)} %get-tuple-element.34, f32[16,1,6,768]{3,0,2,1:T(8,128)} %get-tuple-element.33, f32[16,48,6,1]{3,0,2,1:T(8,128)} %copy.86, f32[16,48,6,1]{3,0,2,1:T(8,128)} %copy.85, f32[48,6,768]{2,1,0:T(8,128)} %copy.75, ...), kind=kLoop, calls=%fused_computation.20 | loop fusion | flops 53084160 | bytes 32477184 | tf_op jit(solution)/shard_map/add | solution.py:78
  404.7 5.3 fusion.56
  412.2 3.4 copy.88
  415.6 3.4 copy.89
  430.5 26.3 %collective-permute-done.13 = f32[16,6,4,768]{3,0,2,1:T(8,128)S(1)} collective-permute-done((f32[16,6,4,768]{3,0,2,1:T(8,128)S(1)}, f32[16,6,4,768]{3,0,2,1:T(8,128)S(1)}, u32[]{:S(2)}, u32[]{:S(2)}) %collective-permute-start.13) | collective-permute-done | bytes 1179680 | tf_op jit(solution)/shard_map/ppermute | solution.py:44
  458.1 26.4 %collective-permute-done.14 = f32[16,6,4,768]{3,0,2,1:T(8,128)S(1)} collective-permute-done((f32[16,6,4,768]{3,0,2,1:T(8,128)S(1)}, f32[16,6,4,768]{3,0,2,1:T(8,128)S(1)}, u32[]{:S(2)}, u32[]{:S(2)}) %collective-permute-start.14) | collective-permute-done | bytes 1179680 | tf_op jit(solution)/shard_map/ppermute | solution.py:44
  490.6 46.9 %collective-permute-done.15 = f32[16,6,4,768]{3,0,2,1:T(8,128)S(1)} collective-permute-done((f32[16,6,4,768]{3,0,2,1:T(8,128)S(1)}, f32[16,6,4,768]{3,0,2,1:T(8,128)S(1)}, u32[]{:S(2)}, u32[]{:S(2)}) %collective-permute-start.15) | collective-permute-done | bytes 1179680 | tf_op jit(solution)/shard_map/ppermute | solution.py:44
  545.3 4.7 rev.11
  553.8 4.0 copy.94
  557.8 4.0 copy.95
  563.3 35.4 %fusion.4 = f32[16,48,6,768]{3,0,2,1:T(8,128)} fusion(f32[16,48,6,768]{3,0,2,1:T(8,128)} %fusion.15, f32[16,1,6,768]{3,0,2,1:T(8,128)S(1)} %get-tuple-element.30, f32[16,1,6,768]{3,0,2,1:T(8,128)S(1)} %get-tuple-element.29, f32[16,48,6,1]{3,0,2,1:T(8,128)} %copy.95, f32[16,48,6,1]{3,0,2,1:T(8,128)} %copy.94, f32[16]{0:T(128)S(1)} %copy-done.10, ...), kind=kLoop, calls=%fused_computation.5 | loop fusion | flops 67239936 | bytes 46633088 | tf_op jit(solution)/shard_map/add | solution.py:89
  598.7 18.5 %copy.96 = f32[16,48,6,768]{3,1,2,0:T(8,128)} copy(f32[16,48,6,768]{3,0,2,1:T(8,128)} %fusion.4) | data formatting | bytes 28311552 | tf_op jit(solution)/shard_map/add | solution.py:89
  (114 shorter events, 110.6 us)
Async XLA Ops:
  29.0 4.6 collective-permute-start
  33.8 29.2 %collective-permute-start.1 = (f32[16,6,4,768]{3,0,2,1:T(8,128)S(1)}, f32[16,6,4,768]{3,0,2,1:T(8,128)S(1)}, u32[]{:S(2)}, u32[]{:S(2)}) collective-permute-start(f32[16,6,4,768]{3,0,2,1:T(8,128)S(1)} %fusion.54), channel_id=1, source_target_pairs={{0,2},{1,3},{2,0},{3,1},{4,6},{5,7},{6,4},{7,5},{8,10},{9,11},{10,... | collective-permute-start | bytes 3538952 | tf_op jit(solution)/shard_map/ppermute | solution.py:44
  63.0 35.1 %copy-start.9 = (s32[6,4,3]{0,1,2:T(4,128)S(1)}, s32[6,4,3]{0,1,2:T(4,128)}, u32[]{:S(2)}) copy-start(s32[6,4,3]{0,1,2:T(4,128)} %param.9) | copy-start | bytes 868
  63.3 35.0 %copy-start.8 = (f32[4,48,6,768]{3,1,2,0:T(8,128)S(1)}, f32[4,48,6,768]{3,1,2,0:T(8,128)}, u32[]{:S(2)}) copy-start(f32[4,48,6,768]{3,1,2,0:T(8,128)} %param.8) | copy-start | bytes 10616836
  63.3 27.5 %collective-permute-start.2 = (f32[16,6,4,768]{3,0,2,1:T(8,128)S(1)}, f32[16,6,4,768]{3,0,2,1:T(8,128)S(1)}, u32[]{:S(2)}, u32[]{:S(2)}) collective-permute-start(f32[16,6,4,768]{3,0,2,1:T(8,128)S(1)} %fusion.69), channel_id=1, source_target_pairs={{0,4},{1,5},{2,6},{3,7},{4,0},{5,1},{6,2},{7,3},{8,12},{9,13},{10,... | collective-permute-start | bytes 3538952 | tf_op jit(solution)/shard_map/ppermute | solution.py:44
  92.0 53.1 %collective-permute-start.3 = (f32[16,6,4,768]{3,0,2,1:T(8,128)}, f32[16,6,4,768]{3,0,2,1:T(8,128)}, u32[]{:S(2)}, u32[]{:S(2)}) collective-permute-start(f32[16,6,4,768]{3,0,2,1:T(8,128)} %add.92), channel_id=1, source_target_pairs={{0,8},{1,9},{2,10},{3,11},{4,12},{5,13},{6,14},{7,15},{8,0},{9,1},... | collective-permute-start | bytes 3538952 | tf_op jit(solution)/shard_map/ppermute | solution.py:44
  94.6 78.6 %collective-permute-start.4 = (f32[16,1,6,768]{3,0,2,1:T(8,128)}, f32[16,1,6,768]{3,0,2,1:T(8,128)}, u32[]{:S(2)}, u32[]{:S(2)}) collective-permute-start(f32[16,1,6,768]{3,0,2,1:T(8,128)} %get-tuple-element.17), channel_id=1, source_target_pairs={{0,1},{1,2},{2,3},{3,4},{4,5},{5,6},{6,7},{7,8},{8,9},{9,10},{10,1... | collective-permute-start | bytes 884744 | tf_op jit(solution)/shard_map/ppermute | solution.py:15
  96.6 76.6 %collective-permute-start.5 = (f32[16,1,6,768]{3,0,2,1:T(8,128)}, f32[16,1,6,768]{3,0,2,1:T(8,128)}, u32[]{:S(2)}, u32[]{:S(2)}) collective-permute-start(f32[16,1,6,768]{3,0,2,1:T(8,128)} %get-tuple-element.19), channel_id=1, source_target_pairs={{1,0},{2,1},{3,2},{4,3},{5,4},{6,5},{7,6},{8,7},{9,8},{10,9},{11,1... | collective-permute-start | bytes 884744 | tf_op jit(solution)/shard_map/ppermute | solution.py:17
  161.1 1.0 copy-start.6
  227.1 1.2 copy-start.3
  227.1 1.2 copy-start.4
  228.4 3.6 collective-permute-start.6
  232.2 28.5 %collective-permute-start.7 = (f32[16,6,4,768]{3,0,1,2:T(8,128)S(1)}, f32[16,6,4,768]{3,0,1,2:T(8,128)S(1)}, u32[]{:S(2)}, u32[]{:S(2)}) collective-permute-start(f32[16,6,4,768]{3,0,1,2:T(8,128)S(1)} %fusion.53), channel_id=1, source_target_pairs={{0,2},{1,3},{2,0},{3,1},{4,6},{5,7},{6,4},{7,5},{8,10},{9,11},{10,... | collective-permute-start | bytes 3538952 | tf_op jit(solution)/shard_map/ppermute | solution.py:44
  261.0 27.5 %collective-permute-start.8 = (f32[16,6,4,768]{3,0,1,2:T(8,128)S(1)}, f32[16,6,4,768]{3,0,1,2:T(8,128)S(1)}, u32[]{:S(2)}, u32[]{:S(2)}) collective-permute-start(f32[16,6,4,768]{3,0,1,2:T(8,128)S(1)} %fusion.68), channel_id=1, source_target_pairs={{0,4},{1,5},{2,6},{3,7},{4,0},{5,1},{6,2},{7,3},{8,12},{9,13},{10,... | collective-permute-start | bytes 3538952 | tf_op jit(solution)/shard_map/ppermute | solution.py:44
  288.6 52.8 %collective-permute-start.9 = (f32[16,6,4,768]{3,0,1,2:T(8,128)S(1)}, f32[16,6,4,768]{3,0,1,2:T(8,128)S(1)}, u32[]{:S(2)}, u32[]{:S(2)}) collective-permute-start(f32[16,6,4,768]{3,0,1,2:T(8,128)S(1)} %add.101), channel_id=1, source_target_pairs={{0,8},{1,9},{2,10},{3,11},{4,12},{5,13},{6,14},{7,15},{8,0},{9,1},... | collective-permute-start | bytes 3538952 | tf_op jit(solution)/shard_map/ppermute | solution.py:44
  291.1 77.0 %collective-permute-start.10 = (f32[16,1,6,768]{3,0,2,1:T(8,128)}, f32[16,1,6,768]{3,0,2,1:T(8,128)}, u32[]{:S(2)}, u32[]{:S(2)}) collective-permute-start(f32[16,1,6,768]{3,0,2,1:T(8,128)} %get-tuple-element.11), channel_id=1, source_target_pairs={{0,1},{1,2},{2,3},{3,4},{4,5},{5,6},{6,7},{7,8},{8,9},{9,10},{10,1... | collective-permute-start | bytes 884744 | tf_op jit(solution)/shard_map/ppermute | solution.py:15
  293.1 75.0 %collective-permute-start.11 = (f32[16,1,6,768]{3,0,2,1:T(8,128)}, f32[16,1,6,768]{3,0,2,1:T(8,128)}, u32[]{:S(2)}, u32[]{:S(2)}) collective-permute-start(f32[16,1,6,768]{3,0,2,1:T(8,128)} %get-tuple-element.14), channel_id=1, source_target_pairs={{1,0},{2,1},{3,2},{4,3},{5,4},{6,5},{7,6},{8,7},{9,8},{10,9},{11,1... | collective-permute-start | bytes 884744 | tf_op jit(solution)/shard_map/ppermute | solution.py:17
  356.1 1.0 copy-start.7
  423.1 1.2 copy-start.1
  423.1 1.2 copy-start.2
  424.4 3.7 collective-permute-start.12
  428.3 28.5 %collective-permute-start.13 = (f32[16,6,4,768]{3,0,2,1:T(8,128)S(1)}, f32[16,6,4,768]{3,0,2,1:T(8,128)S(1)}, u32[]{:S(2)}, u32[]{:S(2)}) collective-permute-start(f32[16,6,4,768]{3,0,2,1:T(8,128)S(1)} %fusion.52), channel_id=1, source_target_pairs={{0,2},{1,3},{2,0},{3,1},{4,6},{5,7},{6,4},{7,5},{8,10},{9,11},{10,... | collective-permute-start | bytes 3538952 | tf_op jit(solution)/shard_map/ppermute | solution.py:44
  457.0 27.5 %collective-permute-start.14 = (f32[16,6,4,768]{3,0,2,1:T(8,128)S(1)}, f32[16,6,4,768]{3,0,2,1:T(8,128)S(1)}, u32[]{:S(2)}, u32[]{:S(2)}) collective-permute-start(f32[16,6,4,768]{3,0,2,1:T(8,128)S(1)} %fusion.67), channel_id=1, source_target_pairs={{0,4},{1,5},{2,6},{3,7},{4,0},{5,1},{6,2},{7,3},{8,12},{9,13},{10,... | collective-permute-start | bytes 3538952 | tf_op jit(solution)/shard_map/ppermute | solution.py:44
  484.7 52.8 %collective-permute-start.15 = (f32[16,6,4,768]{3,0,2,1:T(8,128)S(1)}, f32[16,6,4,768]{3,0,2,1:T(8,128)S(1)}, u32[]{:S(2)}, u32[]{:S(2)}) collective-permute-start(f32[16,6,4,768]{3,0,2,1:T(8,128)S(1)} %add.108), channel_id=1, source_target_pairs={{0,8},{1,9},{2,10},{3,11},{4,12},{5,13},{6,14},{7,15},{8,0},{9,1},... | collective-permute-start | bytes 3538952 | tf_op jit(solution)/shard_map/ppermute | solution.py:44
  487.1 74.6 %collective-permute-start.16 = (f32[16,1,6,768]{3,0,2,1:T(8,128)}, f32[16,1,6,768]{3,0,2,1:T(8,128)}, u32[]{:S(2)}, u32[]{:S(2)}) collective-permute-start(f32[16,1,6,768]{3,0,2,1:T(8,128)} %get-tuple-element.5), channel_id=1, source_target_pairs={{0,1},{1,2},{2,3},{3,4},{4,5},{5,6},{6,7},{7,8},{8,9},{9,10},{10,1... | collective-permute-start | bytes 884744 | tf_op jit(solution)/shard_map/ppermute | solution.py:15
  489.1 72.7 %collective-permute-start.17 = (f32[16,1,6,768]{3,0,2,1:T(8,128)}, f32[16,1,6,768]{3,0,2,1:T(8,128)}, u32[]{:S(2)}, u32[]{:S(2)}) collective-permute-start(f32[16,1,6,768]{3,0,2,1:T(8,128)} %get-tuple-element.8), channel_id=1, source_target_pairs={{1,0},{2,1},{3,2},{4,3},{5,4},{6,5},{7,6},{8,7},{9,8},{10,9},{11,1... | collective-permute-start | bytes 884744 | tf_op jit(solution)/shard_map/ppermute | solution.py:17
  552.0 1.0 copy-start.5
  561.7 1.5 copy-start
  561.7 1.5 copy-start.10
  561.8 1.5 copy-start.11
